TPU v7x, 128 devices: a whole 4x4x4 slice. The times are simulated.
128 devices in a mesh: pair: 8 (over x, core), ints: 16 (over y, z).
Axes of the slice: x: 4, y: 4, z: 4, core: 2. Of those that a mesh axis runs over, the one named last changes fastest.
Arguments:
- t2: bfloat16 [4096, 8192], P('pair', 'ints'), may hold values from -6 to 6
- t2_live: int32 [8, 64], P('pair', 'ints'), may hold values 0 or 1
- int_tiles: int32 [5120, 2], P('ints'), may hold values from 0 to 63
- integrals: bfloat16 [5120, 128, 128], P('ints'), may hold values from -0.0625 to 0.0625
- cycle_w: bfloat16 [4096, 4096], P('pair'), may hold values from -0.09375 to 0.09375
- res_live: int32 [8, 64], P('pair', 'ints'), may hold values 0 or 1
Outputs:
- residual: float32 [4096, 8192], P('pair', 'ints')
All inputs are finite; a program needn't handle non-finite values. No bound on the sum of `t2_live` or of `res_live` on one device may be relied on, other than what follows from the above.
Results may differ from a plain program's by a relative error of at most 0.0003.
Values may be sent and summed in bfloat16 or wider, within the bound.
No kernel may reach another device: no remote copies, remote signals or barrier semaphores. Data moves between devices by JAX's collectives and lax.ppermute only.
A program may use at most 192 MiB of HBM per device.

v0:
```python
import jax
import jax.numpy as jnp
from jax import lax
from jax.sharding import PartitionSpec as P


def local(t2, t2_live, int_tiles, integrals, cycle_w, res_live):
    rows_here = t2.shape[0]
    tile_size = integrals.shape[1]
    tiles_here = t2.shape[1] // tile_size
    live_mask = t2_live[0].astype(t2.dtype)
    amps = (t2.reshape(rows_here, tiles_here, tile_size) * live_mask[None, :, None]).reshape(
        rows_here, tiles_here * tile_size
    )
    block_amps = lax.all_gather(amps, "ints", axis=1, tiled=True)
    tiles_all = block_amps.shape[1] // tile_size
    amps_tiled = block_amps.reshape(rows_here, tiles_all, tile_size)
    count_here = integrals.shape[0]
    group_size = 64
    tile_groups = int_tiles.reshape(count_here // group_size, group_size, 2)
    int_groups = integrals.reshape(count_here // group_size, group_size, tile_size, tile_size)
    tile_ids = jnp.arange(tiles_all, dtype=jnp.int32)

    def ladder_step(partial_value, entry):
        pairs_uv, blocks = entry
        source_table = (pairs_uv[:, 0:1] == tile_ids[None, :]).astype(jnp.bfloat16)
        target_table = (pairs_uv[:, 1:2] == tile_ids[None, :]).astype(jnp.float32)
        picked = jnp.einsum(
            "jt,ptc->jpc", source_table, amps_tiled, preferred_element_type=jnp.float32
        ).astype(jnp.bfloat16)
        product = jnp.einsum("jpc,jcd->jpd", picked, blocks, preferred_element_type=jnp.float32)
        partial_value = partial_value + jnp.einsum(
            "jv,jpd->vpd", target_table, product, precision=lax.Precision.HIGHEST
        )
        return (partial_value, None)

    start_sum = jnp.zeros((tiles_all, rows_here, tile_size), jnp.float32)
    partial_value, _ = lax.scan(ladder_step, start_sum, (tile_groups, int_groups))
    summed = lax.psum(partial_value, "ints")
    owned = lax.dynamic_slice_in_dim(summed, lax.axis_index("ints") * tiles_here, tiles_here, 0)
    ladder = owned.transpose(1, 0, 2).reshape(rows_here, tiles_here * tile_size)
    cycle_term = jnp.dot(
        cycle_w,
        lax.all_gather(amps, "pair", axis=0, tiled=True),
        preferred_element_type=jnp.float32,
    )
    keep_mask = jnp.repeat(res_live[0], tile_size).astype(jnp.float32)[None, :]
    return keep_mask * (ladder + cycle_term)


def solution(mesh):
    placed = (
        P("pair", "ints"),
        P("pair", "ints"),
        P("ints", None),
        P("ints", None, None),
        P("pair", None),
        P("pair", "ints"),
    )
    return jax.shard_map(
        local, mesh=mesh, in_specs=placed, out_specs=P("pair", "ints"), check_vma=False
    )
```

profile of v0, /device:TPU:1, one launch (start us, length us, event | category | flops | bytes accessed | tf_op | source)
XLA Modules:
  0.0 551.5 jit_solution(12331240370962497261)
XLA Ops:
  7.4 0.7 convert_bitcast_fusion
  8.0 0.1 broadcast_bitcast_fusion.1
  8.1 1.9 broadcast_multiply_fusion
  10.0 0.0 all-reduce.2.cloned.1.call-start
  10.1 0.8 reshape.30
  10.8 80.4 %all-gather.3.cloned.1.call-done = bf16[512,8192]{1,0:T(8,128)(2,1)} async-done(((bf16[512,512]{1,0:T(8,128)(2,1)}), bf16[512,8192]{1,0:T(8,128)(2,1)}) %all-gather.3.cloned.1.call-update) | async-done | bytes 8388624 | tf_op jit(solution)/shard_map/all_gather | solution.py:15
  91.2 9.3 %copy.15 = bf16[64,8,64,128]{3,2,1,0:T(8,128)(2,1)} copy(bf16[64,8,64,128]{3,1,2,0:T(8,128)(2,1)} %bitcast.55) | data formatting | bytes 16777216
  100.5 213.6 %while.12 = (s32[]{:T(128)}, f32[64,512,128]{2,0,1:T(8,128)}, s32[5,64,2]{1,0,2:T(8,128)S(1)}, bf16[512,64,128]{2,1,0:T(8,128)(2,1)}, bf16[5,64,128,128]{3,2,1,0:T(8,128)(2,1)}, /*index=5*/s32[]{:T(128)}, s32[]{:T(128)}) while((s32[]{:T(128)}, f32[64,512,128]{2,0,1:T(8,128)}, s32[5,64,2]{1,0,2:T(8,128)S(1)}, ...), condition=%wide.region_1.2_spmd.clone.clone, body=%wide.region_0.1_spmd.clone.clone.sunk | while | flops 4840235008 | bytes 94374496 | solution.py:38
  100.5 5.8 %fusion.34 = bf16[64,512,128]{2,0,1:T(8,128)(2,1)S(1)} fusion(bf16[512,64,128]{2,1,0:T(8,128)(2,1)} %get-tuple-element.146, s32[64]{0:T(128)S(1)} %get-tuple-element.127), kind=kOutput, calls=%fused_computation.12.clone.1 | convolution fusion | flops 536875008 | bytes 16777472 | tf_op jit(solution)/shard_map/while/body/eval_jaxpr/jt,ptc->jpc/dot_general | solution.py:28
  106.3 13.9 %fusion.35 = f32[64,512,128]{2,1,0:T(8,128)} fusion(bf16[64,512,128]{2,0,1:T(8,128)(2,1)S(1)} %fusion.34, bf16[5,64,128,128]{3,2,1,0:T(8,128)(2,1)} %get-tuple-element.147, s32[]{:T(128)S(6)} %copy.28), kind=kOutput, calls=%fused_computation.5.clone.1 | convolution fusion | flops 1073741824 | bytes 27262980 | tf_op jit(solution)/shard_map/while/body/eval_jaxpr/jpc,jcd->jpd/dot_general | solution.py:31
  120.2 20.4 %select_add_fusion.2 = f32[64,512,128]{2,0,1:T(8,128)} fusion(f32[64,512,128]{2,0,1:T(8,128)} %get-tuple-element.137, f32[64,512,128]{2,1,0:T(8,128)} %fusion.35, pred[]{:T(512)S(6)} %compare.3, s32[64]{0:T(128)S(1)} %get-tuple-element.128), kind=kOutput, calls=%fused_computation.4.clone.1 | convolution fusion | flops 3229618176 | bytes 50331904 | tf_op jit(solution)/shard_map/while/body/eval_jaxpr/jv,jpd->vpd/dot_general | solution.py:32
  140.6 5.8 %fusion.34 = bf16[64,512,128]{2,0,1:T(8,128)(2,1)S(1)} fusion(bf16[512,64,128]{2,1,0:T(8,128)(2,1)} %get-tuple-element.146, s32[64]{0:T(128)S(1)} %get-tuple-element.127), kind=kOutput, calls=%fused_computation.12.clone.1 | convolution fusion | flops 536875008 | bytes 16777472 | tf_op jit(solution)/shard_map/while/body/eval_jaxpr/jt,ptc->jpc/dot_general | solution.py:28
  146.4 13.9 %fusion.35 = f32[64,512,128]{2,1,0:T(8,128)} fusion(bf16[64,512,128]{2,0,1:T(8,128)(2,1)S(1)} %fusion.34, bf16[5,64,128,128]{3,2,1,0:T(8,128)(2,1)} %get-tuple-element.147, s32[]{:T(128)S(6)} %copy.28), kind=kOutput, calls=%fused_computation.5.clone.1 | convolution fusion | flops 1073741824 | bytes 27262980 | tf_op jit(solution)/shard_map/while/body/eval_jaxpr/jpc,jcd->jpd/dot_general | solution.py:31
  160.3 23.7 %select_add_fusion.2 = f32[64,512,128]{2,0,1:T(8,128)} fusion(f32[64,512,128]{2,0,1:T(8,128)} %get-tuple-element.137, f32[64,512,128]{2,1,0:T(8,128)} %fusion.35, pred[]{:T(512)S(6)} %compare.3, s32[64]{0:T(128)S(1)} %get-tuple-element.128), kind=kOutput, calls=%fused_computation.4.clone.1 | convolution fusion | flops 3229618176 | bytes 50331904 | tf_op jit(solution)/shard_map/while/body/eval_jaxpr/jv,jpd->vpd/dot_general | solution.py:32
  184.0 5.8 %fusion.34 = bf16[64,512,128]{2,0,1:T(8,128)(2,1)S(1)} fusion(bf16[512,64,128]{2,1,0:T(8,128)(2,1)} %get-tuple-element.146, s32[64]{0:T(128)S(1)} %get-tuple-element.127), kind=kOutput, calls=%fused_computation.12.clone.1 | convolution fusion | flops 536875008 | bytes 16777472 | tf_op jit(solution)/shard_map/while/body/eval_jaxpr/jt,ptc->jpc/dot_general | solution.py:28
  189.8 13.9 %fusion.35 = f32[64,512,128]{2,1,0:T(8,128)} fusion(bf16[64,512,128]{2,0,1:T(8,128)(2,1)S(1)} %fusion.34, bf16[5,64,128,128]{3,2,1,0:T(8,128)(2,1)} %get-tuple-element.147, s32[]{:T(128)S(6)} %copy.28), kind=kOutput, calls=%fused_computation.5.clone.1 | convolution fusion | flops 1073741824 | bytes 27262980 | tf_op jit(solution)/shard_map/while/body/eval_jaxpr/jpc,jcd->jpd/dot_general | solution.py:31
  203.7 23.7 %select_add_fusion.2 = f32[64,512,128]{2,0,1:T(8,128)} fusion(f32[64,512,128]{2,0,1:T(8,128)} %get-tuple-element.137, f32[64,512,128]{2,1,0:T(8,128)} %fusion.35, pred[]{:T(512)S(6)} %compare.3, s32[64]{0:T(128)S(1)} %get-tuple-element.128), kind=kOutput, calls=%fused_computation.4.clone.1 | convolution fusion | flops 3229618176 | bytes 50331904 | tf_op jit(solution)/shard_map/while/body/eval_jaxpr/jv,jpd->vpd/dot_general | solution.py:32
  227.4 5.8 %fusion.34 = bf16[64,512,128]{2,0,1:T(8,128)(2,1)S(1)} fusion(bf16[512,64,128]{2,1,0:T(8,128)(2,1)} %get-tuple-element.146, s32[64]{0:T(128)S(1)} %get-tuple-element.127), kind=kOutput, calls=%fused_computation.12.clone.1 | convolution fusion | flops 536875008 | bytes 16777472 | tf_op jit(solution)/shard_map/while/body/eval_jaxpr/jt,ptc->jpc/dot_general | solution.py:28
  233.1 13.9 %fusion.35 = f32[64,512,128]{2,1,0:T(8,128)} fusion(bf16[64,512,128]{2,0,1:T(8,128)(2,1)S(1)} %fusion.34, bf16[5,64,128,128]{3,2,1,0:T(8,128)(2,1)} %get-tuple-element.147, s32[]{:T(128)S(6)} %copy.28), kind=kOutput, calls=%fused_computation.5.clone.1 | convolution fusion | flops 1073741824 | bytes 27262980 | tf_op jit(solution)/shard_map/while/body/eval_jaxpr/jpc,jcd->jpd/dot_general | solution.py:31
  247.1 23.7 %select_add_fusion.2 = f32[64,512,128]{2,0,1:T(8,128)} fusion(f32[64,512,128]{2,0,1:T(8,128)} %get-tuple-element.137, f32[64,512,128]{2,1,0:T(8,128)} %fusion.35, pred[]{:T(512)S(6)} %compare.3, s32[64]{0:T(128)S(1)} %get-tuple-element.128), kind=kOutput, calls=%fused_computation.4.clone.1 | convolution fusion | flops 3229618176 | bytes 50331904 | tf_op jit(solution)/shard_map/while/body/eval_jaxpr/jv,jpd->vpd/dot_general | solution.py:32
  270.7 5.8 %fusion.34 = bf16[64,512,128]{2,0,1:T(8,128)(2,1)S(1)} fusion(bf16[512,64,128]{2,1,0:T(8,128)(2,1)} %get-tuple-element.146, s32[64]{0:T(128)S(1)} %get-tuple-element.127), kind=kOutput, calls=%fused_computation.12.clone.1 | convolution fusion | flops 536875008 | bytes 16777472 | tf_op jit(solution)/shard_map/while/body/eval_jaxpr/jt,ptc->jpc/dot_general | solution.py:28
  276.5 13.9 %fusion.35 = f32[64,512,128]{2,1,0:T(8,128)} fusion(bf16[64,512,128]{2,0,1:T(8,128)(2,1)S(1)} %fusion.34, bf16[5,64,128,128]{3,2,1,0:T(8,128)(2,1)} %get-tuple-element.147, s32[]{:T(128)S(6)} %copy.28), kind=kOutput, calls=%fused_computation.5.clone.1 | convolution fusion | flops 1073741824 | bytes 27262980 | tf_op jit(solution)/shard_map/while/body/eval_jaxpr/jpc,jcd->jpd/dot_general | solution.py:31
  290.4 23.7 %select_add_fusion.2 = f32[64,512,128]{2,0,1:T(8,128)} fusion(f32[64,512,128]{2,0,1:T(8,128)} %get-tuple-element.137, f32[64,512,128]{2,1,0:T(8,128)} %fusion.35, pred[]{:T(512)S(6)} %compare.3, s32[64]{0:T(128)S(1)} %get-tuple-element.128), kind=kOutput, calls=%fused_computation.4.clone.1 | convolution fusion | flops 3229618176 | bytes 50331904 | tf_op jit(solution)/shard_map/while/body/eval_jaxpr/jv,jpd->vpd/dot_general | solution.py:32
  314.1 0.2 all-gather.5.cloned.1.call-start
  314.4 0.3 all-gather.5.cloned.1.call-update
  314.7 0.0 copy-done
  314.8 0.1 broadcast_bitcast_fusion
  314.8 219.9 %all-reduce.2.cloned.1.call-done = f32[64,512,128]{2,0,1:T(8,128)} async-done(((f32[64,512,128]{2,0,1:T(8,128)}), f32[64,512,128]{2,0,1:T(8,128)}) %all-reduce.2.cloned.1.call-update) | async-done | bytes 16777232 | tf_op jit(solution)/shard_map/psum | solution.py:39
  534.7 1.8 dynamic-slice_bitcast_fusion
  536.5 0.4 copy.10
  536.9 5.8 %fusion.18 = f32[512,512]{0,1:T(8,128)S(1)} fusion(f32[512,512]{0,1:T(8,128)S(1)} %bitcast.56, bf16[4096,512]{1,0:T(8,128)(2,1)} %all-gather.5.cloned.1.call-done, bf16[512,4096]{1,0:T(8,128)(2,1)} %param.12, f32[512]{0:T(512)S(1)} %broadcast_bitcast_fusion), kind=kOutput, calls=%fused_computation.21 | convolution fusion | flops 2148007936 | bytes 10487808 | tf_op jit(solution)/shard_map/dot_general | solution.py:42
  542.8 1.3 copy.11
  (17 shorter events, 0.1 us)
Async XLA Ops:
  7.4 83.8 %all-gather.3.cloned.1.call-start = ((), (), s32[]{:S(2)}) async-start(), calls=%async_computation | async-start | bytes 8912896 | tf_op jit(solution)/shard_map/all_gather | solution.py:15
  10.0 524.7 %all-reduce.2.cloned.1.call-start = ((), (), s32[]{:S(2)}) async-start(), calls=%async_computation.1 | async-start | bytes 33554432 | tf_op jit(solution)/shard_map/psum | solution.py:39
  314.1 0.7 copy-start
  314.1 222.8 %all-gather.5.cloned.1.call-start = ((), (), s32[]{:S(2)}) async-start(), calls=%async_computation.2 | async-start | bytes 4718592 | tf_op jit(solution)/shard_map/all_gather | solution.py:44
Sparse Core Ops, SparseCore 0:
  10.3 80.8 all-gather.2
  314.2 220.4 all-reduce.1
Sparse Core Ops, SparseCore 1:
  316.3 32.4 all-gather.4
where the time goes:
time: 552 us
  waiting for transfers between devices  301 us (55%)
  matrix products  219 us (40%)
  between operations  14.9 us (3%)
  local copies, waits for them, and re-layouts  13.7 us (2%)
    psum x1, waiting for transfers between devices, local(): summed = lax.psum(partial_value, 'ints')  220 us
    dot_general x5, matrix products, ladder_step(): jnp.einsum('jv,jpd->vpd', target_table, product, precision=lax.Precision....  115 us
    all_gather x1, waiting for transfers between devices, local(): block_amps = lax.all_gather(amps, 'ints', axis=1, tiled=True)  80.4 us
    dot_general x5, matrix products, ladder_step(): jnp.einsum('jpc,jcd->jpd', picked, blocks, preferred_element_type=jnp.flo...  69.7 us
    dot_general x5, matrix products, ladder_step(): jnp.einsum('jt,ptc->jpc', source_table, amps_tiled, preferred_element_typ...  28.8 us
  transfers between devices with their start and end apart: 3, of which 2 were waited for; matrix products, arithmetic and copies ran while one was open for 1% of the time, Pallas kernels for 0%

commit v1 on v0

--- a/solution.py
+++ b/solution.py
@@ -36,7 +36,9 @@
 
     start_sum = jnp.zeros((tiles_all, rows_here, tile_size), jnp.float32)
     partial_value, _ = lax.scan(ladder_step, start_sum, (tile_groups, int_groups))
-    summed = lax.psum(partial_value, "ints")
+    summed = partial_value
+    for hop in (1, 2, 4, 8):
+        summed = summed + lax.ppermute(summed, "ints", [(dev, dev ^ hop) for dev in range(16)])
     owned = lax.dynamic_slice_in_dim(summed, lax.axis_index("ints") * tiles_here, tiles_here, 0)
     ladder = owned.transpose(1, 0, 2).reshape(rows_here, tiles_here * tile_size)
     cycle_term = jnp.dot(

time: 552 us -> 1810 us (3.28)
  waiting for transfers between devices: 301 us -> 1510 us
  other arithmetic: 2.53 us -> 41.7 us
    ppermute x0 -> x4, waiting for transfers between devices: none -> 1430 us  [local(): lax.ppermute(summed, 'ints', [(dev, dev ^ hop) for dev in range(16)])]
    psum x1 -> x0, waiting for transfers between devices: 220 us -> none  [local(): summed = lax.psum(partial_value, 'ints')]
    add x0 -> x3, other arithmetic: none -> 36.6 us  [local(): summed + lax.ppermute(summed, 'ints', [(dev, dev ^ hop) for dev in range(...]
  transfers between devices with their start and end apart: 3 -> 6, of which waited for: 2 -> 5; matrix products, arithmetic and copies ran while one was open for 1% -> 0% of each run, Pallas kernels for 0% -> 0%
where the time goes in v1:
time: 1810 us
  waiting for transfers between devices  1510 us (83%)
  matrix products  220 us (12%)
  other arithmetic  41.7 us (2%)
    ppermute x4, waiting for transfers between devices, local(): lax.ppermute(summed, 'ints', [(dev, dev ^ hop) for dev in range(16)])  1430 us
    dot_general x5, matrix products, ladder_step(): jnp.einsum('jv,jpd->vpd', target_table, product, precision=lax.Precision....  115 us
    all_gather x1, waiting for transfers between devices, local(): block_amps = lax.all_gather(amps, 'ints', axis=1, tiled=True)  80.4 us
    dot_general x5, matrix products, ladder_step(): jnp.einsum('jpc,jcd->jpd', picked, blocks, preferred_element_type=jnp.flo...  69.9 us
    add x3, other arithmetic, local(): summed + lax.ppermute(summed, 'ints', [(dev, dev ^ hop) for dev in range(...  36.6 us
  transfers between devices with their start and end apart: 6, of which 5 were waited for; matrix products, arithmetic and copies ran while one was open for 0% of the time, Pallas kernels for 0%

profile of v1, /device:TPU:1, one launch (start us, length us, event | category | flops | bytes accessed | tf_op | source)
XLA Modules:
  0.0 1807.8 jit_solution(11148708350231874698)
XLA Ops:
  8.1 1.9 broadcast_multiply_fusion
  10.8 80.4 %all-gather.3.cloned.1.call-done = bf16[512,8192]{1,0:T(8,128)(2,1)} async-done(((bf16[512,512]{1,0:T(8,128)(2,1)}), bf16[512,8192]{1,0:T(8,128)(2,1)}) %all-gather.3.cloned.1.call-update) | async-done | bytes 8388624 | tf_op jit(solution)/shard_map/all_gather | solution.py:15
  91.2 9.3 copy.15
  100.5 213.9 %while.12 = (s32[]{:T(128)}, f32[64,512,128]{2,0,1:T(8,128)}, s32[5,64,2]{1,0,2:T(8,128)S(1)}, bf16[512,64,128]{2,1,0:T(8,128)(2,1)}, bf16[5,64,128,128]{3,2,1,0:T(8,128)(2,1)}, /*index=5*/s32[]{:T(128)}, s32[]{:T(128)}) while((s32[]{:T(128)}, f32[64,512,128]{2,0,1:T(8,128)}, s32[5,64,2]{1,0,2:T(8,128)S(1)}, ...), condition=%wide.region_1.2_spmd.clone.clone, body=%wide.region_0.1_spmd.clone.clone.sunk | while | flops 4840235008 | bytes 94375000 | solution.py:38
  100.5 5.8 fusion.34
  106.3 14.0 fusion.35
  120.3 20.4 %select_add_fusion.2 = f32[64,512,128]{2,0,1:T(8,128)} fusion(f32[64,512,128]{2,0,1:T(8,128)} %get-tuple-element.137, f32[64,512,128]{2,1,0:T(8,128)} %fusion.35, pred[]{:T(512)S(6)} %compare.3, s32[64]{0:T(128)S(1)} %get-tuple-element.128), kind=kOutput, calls=%fused_computation.4.clone.1 | convolution fusion | flops 3229618176 | bytes 50331904 | tf_op jit(solution)/shard_map/while/body/eval_jaxpr/jv,jpd->vpd/dot_general | solution.py:32
  140.7 5.8 fusion.34
  146.5 14.0 fusion.35
  160.5 23.7 %select_add_fusion.2 = f32[64,512,128]{2,0,1:T(8,128)} fusion(f32[64,512,128]{2,0,1:T(8,128)} %get-tuple-element.137, f32[64,512,128]{2,1,0:T(8,128)} %fusion.35, pred[]{:T(512)S(6)} %compare.3, s32[64]{0:T(128)S(1)} %get-tuple-element.128), kind=kOutput, calls=%fused_computation.4.clone.1 | convolution fusion | flops 3229618176 | bytes 50331904 | tf_op jit(solution)/shard_map/while/body/eval_jaxpr/jv,jpd->vpd/dot_general | solution.py:32
  184.1 5.8 fusion.34
  189.9 14.0 fusion.35
  203.9 23.7 %select_add_fusion.2 = f32[64,512,128]{2,0,1:T(8,128)} fusion(f32[64,512,128]{2,0,1:T(8,128)} %get-tuple-element.137, f32[64,512,128]{2,1,0:T(8,128)} %fusion.35, pred[]{:T(512)S(6)} %compare.3, s32[64]{0:T(128)S(1)} %get-tuple-element.128), kind=kOutput, calls=%fused_computation.4.clone.1 | convolution fusion | flops 3229618176 | bytes 50331904 | tf_op jit(solution)/shard_map/while/body/eval_jaxpr/jv,jpd->vpd/dot_general | solution.py:32
  227.6 5.8 fusion.34
  233.3 14.0 fusion.35
  247.3 23.7 %select_add_fusion.2 = f32[64,512,128]{2,0,1:T(8,128)} fusion(f32[64,512,128]{2,0,1:T(8,128)} %get-tuple-element.137, f32[64,512,128]{2,1,0:T(8,128)} %fusion.35, pred[]{:T(512)S(6)} %compare.3, s32[64]{0:T(128)S(1)} %get-tuple-element.128), kind=kOutput, calls=%fused_computation.4.clone.1 | convolution fusion | flops 3229618176 | bytes 50331904 | tf_op jit(solution)/shard_map/while/body/eval_jaxpr/jv,jpd->vpd/dot_general | solution.py:32
  271.0 5.8 fusion.34
  276.8 14.0 fusion.35
  290.7 23.7 %select_add_fusion.2 = f32[64,512,128]{2,0,1:T(8,128)} fusion(f32[64,512,128]{2,0,1:T(8,128)} %get-tuple-element.137, f32[64,512,128]{2,1,0:T(8,128)} %fusion.35, pred[]{:T(512)S(6)} %compare.3, s32[64]{0:T(128)S(1)} %get-tuple-element.128), kind=kOutput, calls=%fused_computation.4.clone.1 | convolution fusion | flops 3229618176 | bytes 50331904 | tf_op jit(solution)/shard_map/while/body/eval_jaxpr/jv,jpd->vpd/dot_general | solution.py:32
  315.3 359.6 %collective-permute-done = f32[64,512,128]{2,0,1:T(8,128)} collective-permute-done((f32[64,512,128]{2,0,1:T(8,128)}, f32[64,512,128]{2,0,1:T(8,128)}, u32[]{:S(2)}, u32[]{:S(2)}) %collective-permute-start) | collective-permute-done | bytes 16777248 | tf_op jit(solution)/shard_map/ppermute | solution.py:41
  674.9 11.8 add.24
  686.7 2.2 collective-permute-start.1
  688.9 358.7 %collective-permute-done.1 = f32[64,512,128]{2,0,1:T(8,128)} collective-permute-done((f32[64,512,128]{2,0,1:T(8,128)S(1)}, f32[64,512,128]{2,0,1:T(8,128)}, u32[]{:S(2)}, u32[]{:S(2)}) %collective-permute-start.1) | collective-permute-done | bytes 16777248 | tf_op jit(solution)/shard_map/ppermute | solution.py:41
  1047.6 12.4 add.25
  1060.1 0.9 collective-permute-start.2
  1061.0 357.6 %collective-permute-done.2 = f32[64,512,128]{2,0,1:T(8,128)S(1)} collective-permute-done((f32[64,512,128]{2,0,1:T(8,128)}, f32[64,512,128]{2,0,1:T(8,128)S(1)}, u32[]{:S(2)}, u32[]{:S(2)}) %collective-permute-start.2) | collective-permute-done | bytes 16777248 | tf_op jit(solution)/shard_map/ppermute | solution.py:41
  1418.6 12.4 add.26
  1431.0 2.1 collective-permute-start.3
  1433.3 357.0 %collective-permute-done.3 = f32[64,512,128]{2,0,1:T(8,128)} collective-permute-done((f32[64,512,128]{2,0,1:T(8,128)}, f32[64,512,128]{2,0,1:T(8,128)}, u32[]{:S(2)}, u32[]{:S(2)}) %collective-permute-start.3) | collective-permute-done | bytes 16777248 | tf_op jit(solution)/shard_map/ppermute | solution.py:41
  1790.2 2.6 fusion.17
  1793.2 5.8 fusion.18
  1799.1 1.3 copy.11
  (25 shorter events, 3.0 us)
Async XLA Ops:
  7.4 83.8 %all-gather.3.cloned.1.call-start = ((), (), s32[]{:S(2)}) async-start(), calls=%async_computation | async-start | bytes 8912896 | tf_op jit(solution)/shard_map/all_gather | solution.py:15
  10.0 1783.2 %all-gather.5.cloned.1.call-start = ((), (), s32[]{:S(2)}) async-start(), calls=%async_computation.1 | async-start | bytes 4718592 | tf_op jit(solution)/shard_map/all_gather | solution.py:46
  314.4 360.5 %collective-permute-start = (f32[64,512,128]{2,0,1:T(8,128)}, f32[64,512,128]{2,0,1:T(8,128)}, u32[]{:S(2)}, u32[]{:S(2)}) collective-permute-start(f32[64,512,128]{2,0,1:T(8,128)} %get-tuple-element.40), channel_id=1, source_target_pairs={{0,1},{1,0},{2,3},{3,2},{4,5},{5,4},{6,7},{7,6},{8,9},{9,8},{10,11... | collective-permute-start | bytes 50331656 | tf_op jit(solution)/shard_map/ppermute | solution.py:41
  686.7 360.9 %collective-permute-start.1 = (f32[64,512,128]{2,0,1:T(8,128)S(1)}, f32[64,512,128]{2,0,1:T(8,128)}, u32[]{:S(2)}, u32[]{:S(2)}) collective-permute-start(f32[64,512,128]{2,0,1:T(8,128)S(1)} %add.24), channel_id=1, source_target_pairs={{0,2},{1,3},{2,0},{3,1},{4,6},{5,7},{6,4},{7,5},{8,10},{9,11},{10,... | collective-permute-start | bytes 50331656 | tf_op jit(solution)/shard_map/ppermute | solution.py:41
  1060.1 373.1 %copy-start = (s32[1,4]{1,0:T(1,128)S(1)}, s32[1,4]{1,0:T(1,128)}, u32[]{:S(2)}) copy-start(s32[1,4]{1,0:T(1,128)} %param.13) | copy-start | bytes 52
  1060.1 358.5 %collective-permute-start.2 = (f32[64,512,128]{2,0,1:T(8,128)}, f32[64,512,128]{2,0,1:T(8,128)S(1)}, u32[]{:S(2)}, u32[]{:S(2)}) collective-permute-start(f32[64,512,128]{2,0,1:T(8,128)} %add.25), channel_id=1, source_target_pairs={{0,4},{1,5},{2,6},{3,7},{4,0},{5,1},{6,2},{7,3},{8,12},{9,13},{10,... | collective-permute-start | bytes 50331656 | tf_op jit(solution)/shard_map/ppermute | solution.py:41
  1431.0 359.2 %collective-permute-start.3 = (f32[64,512,128]{2,0,1:T(8,128)}, f32[64,512,128]{2,0,1:T(8,128)}, u32[]{:S(2)}, u32[]{:S(2)}) collective-permute-start(f32[64,512,128]{2,0,1:T(8,128)} %add.26), channel_id=1, source_target_pairs={{0,8},{1,9},{2,10},{3,11},{4,12},{5,13},{6,14},{7,15},{8,0},{9,1},... | collective-permute-start | bytes 50331656 | tf_op jit(solution)/shard_map/ppermute | solution.py:41
Sparse Core Ops, SparseCore 0:
  10.3 80.8 all-gather.2
Sparse Core Ops, SparseCore 1:
  1433.3 35.1 all-gather.4
